TPU v7x, 128 devices: a whole 4x4x4 slice. The times are simulated.
128 devices in a mesh: ctx: 32 (over z_lo, y, x), dp: 4 (over z_hi, core).
Axes of the slice: x: 4, y: 4, z: 4 (z_hi: 2, z_lo: 2; z = z_hi * 2 + z_lo), core: 2. Of those that a mesh axis runs over, the one named last changes fastest.
Arguments:
- tokens: bfloat16 [4, 12288, 4096], P('dp', 'ctx'), may hold values from -6 to 6
- key_input: bfloat16 [4, 12288, 2048], P('dp', 'ctx'), may hold values from -6 to 6
- values: bfloat16 [4, 12288, 2048], P('dp', 'ctx'), may hold values from -6 to 6
- q_weight: bfloat16 [4096, 2048], P(('ctx', 'dp')), may hold values from -0.09375 to 0.09375
- q_spikes: int32 [4, 12288, 2048], P('dp', 'ctx'), may hold values 0 or 1
- k_spikes: int32 [4, 12288, 2048], P('dp', 'ctx'), may hold values 0 or 1
- cotangent: bfloat16 [4, 12288, 2048], P('dp', 'ctx'), may hold values from -6 to 6
Outputs:
- attended: bfloat16 [4, 12288, 2048], P('dp', 'ctx')
- grad_tokens: bfloat16 [4, 12288, 4096], P('dp', 'ctx')
- grad_keys: bfloat16 [4, 12288, 2048], P('dp', 'ctx')
- grad_values: bfloat16 [4, 12288, 2048], P('dp', 'ctx')
All inputs are finite; a program needn't handle non-finite values. No bound on the sum of `q_spikes` or of `k_spikes` on one device may be relied on, other than what follows from the above.
Results may differ from a plain program's by a relative error of at most 0.005.
Values may be sent and summed in bfloat16 or wider, within the bound.
A program may use at most 256 MiB of HBM per device.

v0:
```python
import math
import jax
import jax.numpy as jnp
from jax import lax
from jax.sharding import PartitionSpec as P

HEADS = 16
HEAD = 128
exact_mode = lax.Precision.HIGHEST


def entering(part, axis, combine, identity, reverse):
    count = lax.axis_size(axis)
    place = lax.axis_index(axis)
    ahead = count - 1 - place if reverse else place
    gathered = lax.all_gather(part, axis)
    state = jnp.zeros_like(part) + jnp.asarray(identity, part.dtype)

    def one(lap, state):
        source = count - 1 - lap if reverse else lap
        return combine(state, lax.dynamic_index_in_dim(gathered, source, 0, False))

    return lax.fori_loop(0, ahead, one, state)


def add_states(first_part, second_part):
    return first_part + second_part


def per_device(tokens, key_input, values, q_weight, q_spikes, k_spikes, cotangent):
    batches, length, model_width = tokens.shape
    head_total = q_weight.shape[1]
    sequence = length * lax.axis_size("ctx")
    factor = 3.0 / math.sqrt(HEAD * sequence)
    token_rows = tokens.reshape(batches * length, model_width)
    projected = jnp.dot(
        token_rows,
        lax.all_gather(q_weight, ("ctx", "dp"), axis=0, tiled=True),
        preferred_element_type=jnp.float32,
    )
    queries = (
        projected.reshape(batches, length, head_total) * q_spikes.astype(jnp.float32)
    ).astype(jnp.bfloat16)
    spiked_keys = key_input * k_spikes.astype(jnp.bfloat16)

    def by_heads(array):
        return array.reshape(batches, length, HEADS, HEAD)

    query_wide = by_heads(queries)
    key_wide = by_heads(spiked_keys)
    value_wide = by_heads(values)
    grad_wide = by_heads(cotangent)
    wide_float = jnp.float32
    causal = jnp.tril(jnp.ones((length, length), jnp.float32))
    scores = jnp.einsum("blhe,bmhe->bhlm", query_wide, key_wide, preferred_element_type=wide_float)
    scores = (scores * causal).astype(jnp.bfloat16)
    grad_scores = jnp.einsum(
        "blhf,bmhf->bhlm", grad_wide, value_wide, preferred_element_type=wide_float
    )
    grad_scores = (grad_scores * causal).astype(jnp.bfloat16)
    own_memory = jnp.einsum(
        "blhe,blhf->bhef", key_wide, value_wide, preferred_element_type=wide_float
    )
    own_adjoint = jnp.einsum(
        "blhe,blhf->bhef", query_wide, grad_wide, preferred_element_type=wide_float
    )
    zeroes = jnp.zeros_like(own_memory)
    before = entering(own_memory, "ctx", add_states, zeroes, False)
    later_adjoint = entering(own_adjoint, "ctx", add_states, zeroes, True)
    query_float = query_wide.astype(jnp.float32)
    key_float = key_wide.astype(jnp.float32)
    value_float = value_wide.astype(jnp.float32)
    grad_float = grad_wide.astype(jnp.float32)
    output = jnp.einsum("bhlm,bmhf->blhf", scores, value_wide, preferred_element_type=wide_float)
    output = output + jnp.einsum("blhe,bhef->blhf", query_float, before, precision=exact_mode)
    query_grad = jnp.einsum(
        "bhlm,bmhe->blhe", grad_scores, key_wide, preferred_element_type=wide_float
    )
    query_grad = query_grad + jnp.einsum(
        "blhf,bhef->blhe", grad_float, before, precision=exact_mode
    )
    key_grad = jnp.einsum(
        "bhlm,blhe->bmhe", grad_scores, query_wide, preferred_element_type=wide_float
    )
    key_grad = key_grad + jnp.einsum(
        "bmhf,bhef->bmhe", value_float, later_adjoint, precision=exact_mode
    )
    value_grad = jnp.einsum("bhlm,blhf->bmhf", scores, grad_wide, preferred_element_type=wide_float)
    value_grad = value_grad + jnp.einsum(
        "bmhe,bhef->bmhf", key_float, later_adjoint, precision=exact_mode
    )
    shape_out = (batches, length, head_total)
    attended = (factor * output.reshape(shape_out)).astype(jnp.bfloat16)
    masked_grad = (factor * query_grad.reshape(shape_out) * q_spikes.astype(jnp.float32)).astype(
        jnp.bfloat16
    )
    masked_rows = masked_grad.reshape(batches * length, head_total)
    contract = (((1,), (1,)), ((), ()))
    token_grad = lax.dot_general(
        masked_rows,
        lax.all_gather(q_weight, ("ctx", "dp"), axis=0, tiled=True),
        contract,
        preferred_element_type=jnp.float32,
    )
    grad_tokens = token_grad.reshape(batches, length, model_width).astype(jnp.bfloat16)
    grad_keys = (factor * key_grad.reshape(shape_out) * k_spikes.astype(jnp.float32)).astype(
        jnp.bfloat16
    )
    grad_values = (factor * value_grad.reshape(shape_out)).astype(jnp.bfloat16)
    return (attended, grad_tokens, grad_keys, grad_values)


def solution(mesh):
    in_specs = (
        P("dp", "ctx", None),
        P("dp", "ctx", None),
        P("dp", "ctx", None),
        P(("ctx", "dp"), None),
        P("dp", "ctx", None),
        P("dp", "ctx", None),
        P("dp", "ctx", None),
    )
    out_specs = (
        P("dp", "ctx", None),
        P("dp", "ctx", None),
        P("dp", "ctx", None),
        P("dp", "ctx", None),
    )
    return jax.shard_map(
        per_device, mesh=mesh, in_specs=in_specs, out_specs=out_specs, check_vma=False
    )
```

profile of v0, /device:TPU:1, one launch (start us, length us, event | category | flops | bytes accessed | tf_op | source)
XLA Modules:
  0.0 1037.3 jit_solution(814727491231652069)
XLA Ops:
  8.0 2.7 multiply_bitcast_fusion
  10.7 1.6 copy.64
  12.3 2.8 copy.38
  15.1 1.9 copy.65
  18.2 1.8 fusion.25
  20.1 2.6 copy.63
  22.7 204.0 %all-gather.6.cloned.1.call-done = bf16[4096,2048]{1,0:T(8,128)(2,1)} async-done(((bf16[32,2048]{1,0:T(8,128)(2,1)}), bf16[4096,2048]{1,0:T(8,128)(2,1)}) %all-gather.6.cloned.1.call-update) | async-done | bytes 16777232 | tf_op jit(solution)/shard_map/all_gather | solution.py:38
  226.6 12.7 %fusion.5 = bf16[1,384,2048]{2,1,0:T(8,128)(2,1)} fusion(s32[1,384,2048]{2,1,0:T(8,128)} %param.15, bf16[4096,2048]{1,0:T(8,128)(2,1)} %all-gather.6.cloned.1.call-done, bf16[1,384,4096]{2,1,0:T(8,128)(2,1)S(1)} %copy-done), kind=kOutput, calls=%fused_computation.13 | convolution fusion | flops 6444810240 | bytes 24641536 | tf_op jit(solution)/shard_map/dot_general | solution.py:36
  239.3 1.9 copy.62
  241.2 3.4 fusion.28
  244.7 5.7 multiply_convert_fusion
  250.4 4.2 multiply_convert_fusion.1
  254.6 338.1 %all-gather.8.cloned.1.call-done = f32[512,128,128]{2,1,0:T(8,128)} async-done(((f32[16,128,128]{2,1,0:T(8,128)}), f32[512,128,128]{2,1,0:T(8,128)}) %all-gather.8.cloned.1.call-update) | async-done | bytes 33554448 | tf_op jit(solution)/shard_map/all_gather | solution.py:16
  595.3 4.2 fusion.4
  599.5 2.7 copy.57
  602.2 3.0 fusion.18
  605.2 5.7 add_multiply_fusion.1
  610.9 3.6 copy.61
  614.5 13.4 %fusion = bf16[1,384,4096]{2,1,0:T(8,128)(2,1)} fusion(bf16[4096,2048]{1,0:T(8,128)(2,1)} %all-gather.6.cloned.1.call-done, f32[1,384,2048]{2,1,0:T(8,128)} %copy.61, s32[1,384,2048]{2,1,0:T(8,128)} %param.15), kind=kOutput, calls=%fused_computation.5 | convolution fusion | flops 6446383104 | bytes 26214400 | tf_op jit(solution)/shard_map/dot_general | solution.py:99
  627.9 327.8 %all-gather.10.cloned.1.call-done = f32[512,128,128]{2,1,0:T(8,128)} async-done(((f32[16,128,128]{2,1,0:T(8,128)}), f32[512,128,128]{2,1,0:T(8,128)}) %all-gather.10.cloned.1.call-update) | async-done | bytes 33554448 | tf_op jit(solution)/shard_map/all_gather | solution.py:16
  955.8 47.1 %while.23 = (s32[]{:T(128)}, f32[1,16,128,128]{3,2,1,0:T(8,128)S(1)}, s32[]{:T(128)}, f32[32,1,16,128,128]{4,3,2,1,0:T(8,128)}, s32[]{:T(128)}, /*index=5*/s32[]{:T(128)}, s32[]{:T(128)}, s32[]{:T(128)}) while((s32[]{:T(128)}, f32[1,16,128,128]{3,2,1,0:T(8,128)S(1)}, s32[]{:T(128)}, f32[32,1,16,128,128]{4,3,2,1,0:T(8,128)}, s32[]{:T(128)}, ...), condition=%wide.region_3.4_spmd, body=%wide.region_2.3_spmd.sunk | while | flops 262150 | bytes 3145871 | solution.py:23
  955.8 1.5 bitcast_add_fusion.7
  957.3 1.5 bitcast_add_fusion.7
  958.8 1.5 bitcast_add_fusion.7
  960.3 1.5 bitcast_add_fusion.7
  961.9 1.5 bitcast_add_fusion.7
  963.4 1.5 bitcast_add_fusion.7
  964.9 1.5 bitcast_add_fusion.7
  966.4 1.5 bitcast_add_fusion.7
  967.9 1.5 bitcast_add_fusion.7
  969.4 1.5 bitcast_add_fusion.7
  970.9 1.5 bitcast_add_fusion.7
  972.4 1.5 bitcast_add_fusion.7
  974.0 1.5 bitcast_add_fusion.7
  975.5 1.5 bitcast_add_fusion.7
  993.6 1.5 bitcast_add_fusion.7
  995.1 1.5 bitcast_add_fusion.7
  996.6 1.5 bitcast_add_fusion.7
  998.1 1.5 bitcast_add_fusion.7
  999.6 1.5 bitcast_add_fusion.7
  1001.2 1.5 bitcast_add_fusion.7
  1002.9 3.6 fusion.16
  1006.5 3.7 fusion.12
  1010.2 5.3 add_multiply_fusion
  1015.6 3.8 copy.53
  1019.4 3.9 multiply_convert_fusion.2
  1023.3 4.9 fusion.2
  1028.1 2.6 copy.58
  (46 shorter events, 21.2 us)
Async XLA Ops:
  7.2 219.5 %copy-start = (bf16[1,384,4096]{2,1,0:T(8,128)(2,1)S(1)}, bf16[1,384,4096]{2,1,0:T(8,128)(2,1)}, u32[]{:S(2)}) copy-start(bf16[1,384,4096]{2,1,0:T(8,128)(2,1)} %param.11) | copy-start | bytes 9437188
  7.2 219.5 %all-gather.6.cloned.1.call-start = ((), (), s32[]{:S(2)}) async-start(), calls=%async_computation | async-start | bytes 16908288 | tf_op jit(solution)/shard_map/all_gather | solution.py:38
  7.9 584.8 %all-gather.8.cloned.1.call-start = ((), (), s32[]{:S(2)}) async-start(), calls=%async_computation.1 | async-start | bytes 34603008 | tf_op jit(solution)/shard_map/all_gather | solution.py:16
  15.1 3.1 copy-start.8
  17.0 1.2 copy-start.3
  20.0 935.6 %all-gather.10.cloned.1.call-start = ((), (), s32[]{:S(2)}) async-start(), calls=%async_computation.2 | async-start | bytes 34603008 | tf_op jit(solution)/shard_map/all_gather | solution.py:16
  241.2 3.5 copy-start.4
  244.7 5.8 copy-start.6
  593.0 2.3 copy-start.2
  602.2 3.0 copy-start.9
  1002.9 3.6 copy-start.7
  1015.6 3.8 copy-start.10
  1019.4 3.9 copy-start.5
  1019.4 3.9 copy-start.11
  1023.3 7.5 copy-start.1
Sparse Core Ops, SparseCore 0:
  9.7 216.8 all-gather.5
  228.9 363.7 all-gather.7
  594.3 361.3 all-gather.9
where the time goes:
time: 1040 us
  waiting for transfers between devices  870 us (84%)
  matrix products  73 us (7%)
  other arithmetic  52.8 us (5%)
  local copies, waits for them, and re-layouts  25.8 us (2%)
  between operations  13.9 us (1%)
    all_gather x2, waiting for transfers between devices, entering(): gathered = lax.all_gather(part, axis)  666 us
    all_gather x1, waiting for transfers between devices, per_device(): lax.all_gather(q_weight, ('ctx', 'dp'), axis=0, tiled=True)  204 us
    add x31, other arithmetic, add_states(): return first_part + second_part  46.2 us
  transfers between devices with their start and end apart: 3, of which 3 were waited for; matrix products, arithmetic and copies ran while one was open for 7% of the time, Pallas kernels for 0%

commit v1 on v0

--- a/solution.py
+++ b/solution.py
@@ -35,7 +35,12 @@
     token_rows = tokens.reshape(batches * length, model_width)
     projected = jnp.dot(
         token_rows,
-        lax.all_gather(q_weight, ("ctx", "dp"), axis=0, tiled=True),
+        jnp.concatenate(
+            lax.all_to_all(
+                jnp.stack([q_weight] * lax.axis_size(("ctx", "dp"))), ("ctx", "dp"), 0, 0
+            ),
+            axis=0,
+        ),
         preferred_element_type=jnp.float32,
     )
     queries = (

time: 1040 us -> 1240 us (1.19)
  waiting for transfers between devices: 870 us -> 1060 us
    all_to_all x0 -> x1, waiting for transfers between devices: none -> 541 us  [per_device(): lax.all_to_all(jnp.stack([q_weight] * lax.axis_size(('ctx', 'dp'))), ('ct...]
    all_gather x2, waiting for transfers between devices: 666 us -> 352 us  [entering(): gathered = lax.all_gather(part, axis)]
    all_gather x1, waiting for transfers between devices: 204 us -> 164 us  [per_device(): lax.all_gather(q_weight, ('ctx', 'dp'), axis=0, tiled=True)]
  transfers between devices with their start and end apart: 3 -> 4, of which waited for: 3 -> 3; matrix products, arithmetic and copies ran while one was open for 7% -> 6% of each run, Pallas kernels for 0% -> 0%
where the time goes in v1:
time: 1240 us
  waiting for transfers between devices  1060 us (85%)
  matrix products  74.6 us (6%)
  other arithmetic  51.7 us (4%)
  local copies, waits for them, and re-layouts  30 us (2%)
  between operations  13.9 us (1%)
    all_to_all x1, waiting for transfers between devices, per_device(): lax.all_to_all(jnp.stack([q_weight] * lax.axis_size(('ctx', 'dp'))), ('ct...  541 us
    all_gather x2, waiting for transfers between devices, entering(): gathered = lax.all_gather(part, axis)  352 us
    all_gather x1, waiting for transfers between devices, per_device(): lax.all_gather(q_weight, ('ctx', 'dp'), axis=0, tiled=True)  164 us
    add x31, other arithmetic, add_states(): return first_part + second_part  46.1 us
  transfers between devices with their start and end apart: 4, of which 3 were waited for; matrix products, arithmetic and copies ran while one was open for 6% of the time, Pallas kernels for 0%

profile of v1, /device:TPU:1, one launch (start us, length us, event | category | flops | bytes accessed | tf_op | source)
XLA Modules:
  0.0 1242.5 jit_solution(2014253197680028805)
XLA Ops:
  7.2 3.2 copy.65
  10.4 1.7 multiply_bitcast_fusion
  12.1 1.6 copy.64
  13.7 2.8 copy.38
  16.5 3.7 fusion.25
  21.0 6.1 stack.2
  27.1 12.0 all-to-all-start
  39.1 2.6 copy.63
  41.7 541.5 %all-to-all-done = bf16[128,32,2048]{2,1,0:T(8,128)(2,1)} async-done(((bf16[128,32,2048]{2,1,0:T(8,128)(2,1)}), bf16[128,32,2048]{2,1,0:T(8,128)(2,1)}, u32[]{:S(2)}, u32[]{:S(2)}) %all-to-all-start) | async-done | bytes 16777248 | tf_op jit(solution)/shard_map/all_to_all | solution.py:39
  583.2 12.7 %fusion.5 = bf16[1,384,2048]{2,1,0:T(8,128)(2,1)} fusion(s32[1,384,2048]{2,1,0:T(8,128)} %param.15, bf16[4096,2048]{1,0:T(8,128)(2,1)} %bitcast.3, bf16[1,384,4096]{2,1,0:T(8,128)(2,1)S(1)} %copy-done), kind=kOutput, calls=%fused_computation.13 | convolution fusion | flops 6444810240 | bytes 24641536 | tf_op jit(solution)/shard_map/dot_general | solution.py:36
  595.9 1.9 copy.62
  597.8 3.3 fusion.28
  601.2 5.8 multiply_convert_fusion
  607.0 4.2 multiply_convert_fusion.1
  611.5 3.0 fusion.18
  614.5 5.7 add_multiply_fusion.1
  620.3 3.7 copy.61
  625.4 4.0 fusion.4
  629.4 1.6 copy.57
  631.1 164.1 %all-gather.6.cloned.1.call-done = bf16[4096,2048]{1,0:T(8,128)(2,1)} async-done(((bf16[32,2048]{1,0:T(8,128)(2,1)}), bf16[4096,2048]{1,0:T(8,128)(2,1)}) %all-gather.6.cloned.1.call-update) | async-done | bytes 16777232 | tf_op jit(solution)/shard_map/all_gather | solution.py:106
  795.2 13.2 %fusion = bf16[1,384,4096]{2,1,0:T(8,128)(2,1)} fusion(bf16[4096,2048]{1,0:T(8,128)(2,1)} %all-gather.6.cloned.1.call-done, f32[1,384,2048]{2,1,0:T(8,128)} %copy.61, s32[1,384,2048]{2,1,0:T(8,128)} %param.15), kind=kOutput, calls=%fused_computation.5 | convolution fusion | flops 6446383104 | bytes 26214400 | tf_op jit(solution)/shard_map/dot_general | solution.py:104
  808.4 352.5 %all-gather.10.cloned.1.call-done = f32[512,128,128]{2,1,0:T(8,128)} async-done(((f32[16,128,128]{2,1,0:T(8,128)}), f32[512,128,128]{2,1,0:T(8,128)}) %all-gather.10.cloned.1.call-update) | async-done | bytes 33554448 | tf_op jit(solution)/shard_map/all_gather | solution.py:16
  1161.0 47.2 %while.23 = (s32[]{:T(128)}, f32[1,16,128,128]{3,2,1,0:T(8,128)S(1)}, s32[]{:T(128)}, f32[32,1,16,128,128]{4,3,2,1,0:T(8,128)}, s32[]{:T(128)}, /*index=5*/s32[]{:T(128)}, s32[]{:T(128)}, s32[]{:T(128)}) while((s32[]{:T(128)}, f32[1,16,128,128]{3,2,1,0:T(8,128)S(1)}, s32[]{:T(128)}, f32[32,1,16,128,128]{4,3,2,1,0:T(8,128)}, s32[]{:T(128)}, ...), condition=%wide.region_3.4_spmd, body=%wide.region_2.3_spmd.sunk | while | flops 262150 | bytes 3145863 | solution.py:23
  1161.0 1.5 bitcast_add_fusion.7
  1162.5 1.5 bitcast_add_fusion.7
  1164.1 1.5 bitcast_add_fusion.7
  1165.6 1.5 bitcast_add_fusion.7
  1167.1 1.5 bitcast_add_fusion.7
  1168.6 1.5 bitcast_add_fusion.7
  1170.1 1.5 bitcast_add_fusion.7
  1171.6 1.5 bitcast_add_fusion.7
  1173.1 1.5 bitcast_add_fusion.7
  1174.7 1.5 bitcast_add_fusion.7
  1176.2 1.5 bitcast_add_fusion.7
  1177.7 1.5 bitcast_add_fusion.7
  1179.2 1.5 bitcast_add_fusion.7
  1180.7 1.5 bitcast_add_fusion.7
  1182.2 1.5 bitcast_add_fusion.7
  1183.8 1.5 bitcast_add_fusion.7
  1185.3 1.5 bitcast_add_fusion.7
  1186.8 1.5 bitcast_add_fusion.7
  1208.2 3.6 fusion.16
  1211.8 3.7 fusion.12
  1215.6 5.3 add_multiply_fusion
  1220.9 3.7 copy.53
  1224.7 3.9 multiply_convert_fusion.2
  1228.6 4.9 fusion.2
  1233.4 2.6 copy.58
  (49 shorter events, 22.1 us)
Async XLA Ops:
  7.2 576.0 %copy-start = (bf16[1,384,4096]{2,1,0:T(8,128)(2,1)S(1)}, bf16[1,384,4096]{2,1,0:T(8,128)(2,1)}, u32[]{:S(2)}) copy-start(bf16[1,384,4096]{2,1,0:T(8,128)(2,1)} %param.11) | copy-start | bytes 9437188
  7.2 604.0 %all-gather.8.cloned.1.call-start = ((), (), s32[]{:S(2)}) async-start(), calls=%async_computation.2 | async-start | bytes 34603008 | tf_op jit(solution)/shard_map/all_gather | solution.py:16
  7.2 3.2 copy-start.8
  16.5 4.5 copy-start.11
  20.2 774.9 %all-gather.6.cloned.1.call-start = ((), (), s32[]{:S(2)}) async-start(), calls=%async_computation.1 | async-start | bytes 16908288 | tf_op jit(solution)/shard_map/all_gather | solution.py:106
  27.1 556.1 %all-to-all-start = ((bf16[128,32,2048]{2,1,0:T(8,128)(2,1)}), bf16[128,32,2048]{2,1,0:T(8,128)(2,1)}, u32[]{:S(2)}, u32[]{:S(2)}) async-start(bf16[128,32,2048]{2,1,0:T(8,128)(2,1)} %stack.2), calls=%async_computation | async-start | bytes 33554432 | tf_op jit(solution)/shard_map/all_to_all | solution.py:39
  39.1 1121.8 %all-gather.10.cloned.1.call-start = ((), (), s32[]{:S(2)}) async-start(), calls=%async_computation.3 | async-start | bytes 34603008 | tf_op jit(solution)/shard_map/all_gather | solution.py:16
  597.8 3.4 copy-start.2
  601.2 5.8 copy-start.5
  611.5 3.0 copy-start.7
  623.9 1.4 copy-start.3
  1208.2 3.6 copy-start.6
  1220.9 3.7 copy-start.9
  1224.7 3.9 copy-start.4
  1224.7 3.9 copy-start.10
  1228.6 7.5 copy-start.1
Sparse Core Ops, SparseCore 0:
  20.3 555.5 all-gather.7
  577.6 217.4 all-gather.5
  797.4 363.4 all-gather.9
